TPU v7x, 512 devices: a whole 4x8x8 slice. The times are simulated.
512 devices in a mesh: expert: 64 (over z, y), tensor: 8 (over x, core).
Axes of the slice: x: 4, y: 8, z: 8, core: 2. Of those that a mesh axis runs over, the one named last changes fastest.
Arguments:
- tokens: bfloat16 [16384, 2048], P('expert', 'tensor'), may hold values from -6 to 6
- upstream: bfloat16 [16384, 2048], P('expert', 'tensor'), may hold values from -6 to 6
- expert_ids: int32 [16384, 1], P('expert'), may hold values from 0 to 63; in each aligned block of 256 rows (0 to 255, 256 to 511, ...) at most 8 rows name the same one
- w_gate: bfloat16 [64, 1408, 2048], P('expert', 'tensor'), may hold values from -0.125 to 0.125
- w_up: bfloat16 [64, 1408, 2048], P('expert', 'tensor'), may hold values from -0.125 to 0.125
- w_down: bfloat16 [64, 1408, 2048], P('expert', 'tensor'), may hold values from -0.15625 to 0.15625
Outputs:
- grad_tokens: bfloat16 [16384, 2048], P('expert', 'tensor')
- grad_gate: bfloat16 [64, 1408, 2048], P('expert', 'tensor')
- grad_up: bfloat16 [64, 1408, 2048], P('expert', 'tensor')
- grad_down: bfloat16 [64, 1408, 2048], P('expert', 'tensor')
Inputs may be any that keep to these rules, and one draw needn't show every extreme that they name: `expert_ids`: among the 256 tokens of one index of expert, at most 8 name the same expert, and in some such block one expert is named exactly 8 times; every expert is named somewhere.
All inputs are finite; a program needn't handle non-finite values.
Results may differ from a plain program's by a relative error of at most 0.014.
Values may be sent and summed in bfloat16 or wider, within the bound.
A program may use at most 64 MiB of HBM per device.

v0:
```python
import jax
import jax.numpy as jnp
from jax import lax
from jax.sharding import PartitionSpec as P


def on_device(tokens, upstream, expert_ids, w_gate, w_up, w_down):
    experts = lax.axis_size("expert")
    tok_rows = tokens.shape[0]
    capacity = max(2, 2 * tok_rows // experts)
    slot_count = experts * capacity
    route = expert_ids[:, 0]
    onehot = (route[:, None] == jnp.arange(experts, dtype=jnp.int32)[None, :]).astype(jnp.int32)
    before = jnp.cumsum(onehot, axis=0) - onehot
    within = jnp.sum(before * onehot, axis=1)
    target = route * capacity + within
    placing = (target[None, :] == jnp.arange(slot_count, dtype=jnp.int32)[:, None]).astype(
        jnp.bfloat16
    )
    gate_rows = w_gate[0]
    up_rows = w_up[0]
    down_rows = w_down[0]
    full_width = gate_rows.shape[1]

    def spread(values):
        placed = jnp.dot(placing, values, preferred_element_type=jnp.float32).astype(jnp.bfloat16)
        return placed.reshape(experts, capacity, values.shape[1])

    full_x, full_dy = (
        lax.all_gather(tokens, "tensor", axis=1, tiled=True),
        lax.all_gather(upstream, "tensor", axis=1, tiled=True),
    )
    got_x, got_dy = (
        lax.all_to_all(spread(full_x), "expert", split_axis=0, concat_axis=0, tiled=True),
        lax.all_to_all(spread(full_dy), "expert", split_axis=0, concat_axis=0, tiled=True),
    )
    x_all = got_x.reshape(slot_count, full_width)
    dy_all = got_dy.reshape(slot_count, full_width)
    gate_pre = lax.dot_general(
        x_all, gate_rows, (((1,), (1,)), ((), ())), preferred_element_type=jnp.float32
    )
    up_pre = lax.dot_general(
        x_all, up_rows, (((1,), (1,)), ((), ())), preferred_element_type=jnp.float32
    )
    gate_pre, up_pre = (gate_pre, up_pre)
    sig_gate = jax.nn.sigmoid(gate_pre)
    silu_gate = gate_pre * sig_gate
    hidden = (silu_gate * up_pre).astype(jnp.bfloat16)
    d_hidden = lax.dot_general(
        dy_all, down_rows, (((1,), (1,)), ((), ())), preferred_element_type=jnp.float32
    )
    block_grad = lax.dot_general(
        hidden, dy_all, (((0,), (0,)), ((), ())), preferred_element_type=jnp.float32
    )
    down_grad = block_grad
    d_hidden, down_grad = (d_hidden, down_grad)
    d_up = (d_hidden * silu_gate).astype(jnp.bfloat16)
    d_gate = (d_hidden * up_pre * sig_gate * (1.0 + gate_pre * (1.0 - sig_gate))).astype(
        jnp.bfloat16
    )
    grad_gate = lax.dot_general(
        d_gate, x_all, (((0,), (0,)), ((), ())), preferred_element_type=jnp.float32
    ).astype(jnp.bfloat16)
    grad_up = lax.dot_general(
        d_up, x_all, (((0,), (0,)), ((), ())), preferred_element_type=jnp.float32
    ).astype(jnp.bfloat16)
    grad_down = down_grad.astype(jnp.bfloat16)
    partial_rows = jnp.dot(d_gate, gate_rows, preferred_element_type=jnp.float32) + jnp.dot(
        d_up, up_rows, preferred_element_type=jnp.float32
    )
    feat_width = tokens.shape[1]
    totals = lax.psum(partial_rows.astype(jnp.bfloat16), "tensor")
    arrived = lax.all_to_all(
        totals.reshape(experts, capacity, full_width),
        "expert",
        split_axis=0,
        concat_axis=0,
        tiled=True,
    )
    returned = lax.dynamic_slice_in_dim(
        arrived.reshape(slot_count, full_width),
        lax.axis_index("tensor") * feat_width,
        feat_width,
        1,
    )
    grad_tokens = lax.dot_general(
        placing, returned, (((0,), (0,)), ((), ())), preferred_element_type=jnp.float32
    ).astype(jnp.bfloat16)
    return (grad_tokens, grad_gate[None], grad_up[None], grad_down[None])


def solution(mesh):
    in_specs = (
        P("expert", "tensor"),
        P("expert", "tensor"),
        P("expert", None),
        P("expert", "tensor", None),
        P("expert", "tensor", None),
        P("expert", "tensor", None),
    )
    out_specs = (
        P("expert", "tensor"),
        P("expert", "tensor", None),
        P("expert", "tensor", None),
        P("expert", "tensor", None),
    )
    return jax.shard_map(
        on_device, mesh=mesh, in_specs=in_specs, out_specs=out_specs, check_vma=False
    )
```

profile of v0, /device:TPU:15, one launch (start us, length us, event | category | flops | bytes accessed | tf_op | source)
XLA Modules:
  0.0 332.6 jit_solution(9789165003965549662)
XLA Ops:
  7.2 0.0 copy-start
  7.2 0.0 all-gather.5.cloned.1.call-start
  7.2 0.7 all-gather.5.cloned.1.call-update
  7.9 0.7 fusion.29
  8.6 0.6 reduce-window.6
  9.2 0.2 slice_reduce_fusion
  9.4 0.8 fusion.28
  10.2 0.7 multiply_add_fusion
  10.9 32.1 %all-gather.5.cloned.1.call-done = bf16[256,2048]{1,0:T(8,128)(2,1)} async-done(((bf16[256,256]{1,0:T(8,128)(2,1)}), bf16[256,2048]{1,0:T(8,128)(2,1)}) %all-gather.5.cloned.1.call-update) | async-done | bytes 1048592 | tf_op jit(solution)/shard_map/all_gather | solution.py:30
  43.0 3.3 fusion.1
  46.3 12.8 %all-to-all-start.1 = ((bf16[64,8,2048]{2,1,0:T(8,128)(2,1)}), bf16[64,8,2048]{2,1,0:T(8,128)(2,1)S(1)}, u32[]{:S(2)}, u32[]{:S(2)}) async-start(bf16[64,8,2048]{2,1,0:T(8,128)(2,1)} %fusion.1), calls=%async_computation.1 | async-start | bytes 4194304 | tf_op jit(solution)/shard_map/all_to_all | solution.py:34
  59.1 0.0 all-gather.3.cloned.1.call-start
  59.2 0.7 all-gather.3.cloned.1.call-update
  59.9 31.7 %all-gather.3.cloned.1.call-done = bf16[256,2048]{1,0:T(8,128)(2,1)} async-done(((bf16[256,256]{1,0:T(8,128)(2,1)}), bf16[256,2048]{1,0:T(8,128)(2,1)}) %all-gather.3.cloned.1.call-update) | async-done | bytes 1048592 | tf_op jit(solution)/shard_map/all_gather | solution.py:31
  91.6 3.3 fusion
  94.8 15.2 %all-to-all-done.1 = bf16[64,8,2048]{2,1,0:T(8,128)(2,1)S(1)} async-done(((bf16[64,8,2048]{2,1,0:T(8,128)(2,1)}), bf16[64,8,2048]{2,1,0:T(8,128)(2,1)S(1)}, u32[]{:S(2)}, u32[]{:S(2)}) %all-to-all-start.1) | async-done | bytes 2097184 | tf_op jit(solution)/shard_map/all_to_all | solution.py:34
  110.1 9.7 %all-to-all-start = ((bf16[64,8,2048]{2,1,0:T(8,128)(2,1)}), bf16[64,8,2048]{2,1,0:T(8,128)(2,1)}, u32[]{:S(2)}, u32[]{:S(2)}) async-start(bf16[64,8,2048]{2,1,0:T(8,128)(2,1)} %fusion), calls=%async_computation | async-start | bytes 4194304 | tf_op jit(solution)/shard_map/all_to_all | solution.py:35
  119.8 0.0 copy-start.1
  119.8 0.0 all-reduce.2.cloned.1.call-start
  119.9 0.0 copy-done
  119.9 1.6 fusion.8
  121.5 0.0 copy-done.1
  121.5 1.6 fusion.10
  123.0 46.9 %all-to-all-done = bf16[64,8,2048]{2,1,0:T(8,128)(2,1)} async-done(((bf16[64,8,2048]{2,1,0:T(8,128)(2,1)}), bf16[64,8,2048]{2,1,0:T(8,128)(2,1)}, u32[]{:S(2)}, u32[]{:S(2)}) %all-to-all-start) | async-done | bytes 2097184 | tf_op jit(solution)/shard_map/all_to_all | solution.py:35
  170.0 2.8 multiply_convert_fusion.1
  172.8 0.0 copy-start.2
  172.9 0.7 fusion.15
  173.6 0.4 copy-done.2
  174.0 2.1 fusion.2
  176.0 0.0 all-reduce.2.cloned.1.call-update
  176.1 77.0 %all-reduce.2.cloned.1.call-done = bf16[64,8,2048]{2,1,0:T(8,128)(2,1)} async-done(((bf16[64,8,2048]{2,1,0:T(8,128)(2,1)}), bf16[64,8,2048]{2,1,0:T(8,128)(2,1)}) %all-reduce.2.cloned.1.call-update) | async-done | bytes 2097168 | tf_op jit(solution)/shard_map/psum | solution.py:72
  253.1 13.0 %all-to-all-start.2 = ((bf16[64,8,2048]{2,1,0:T(8,128)(2,1)}), bf16[64,8,2048]{2,1,0:T(8,128)(2,1)}, u32[]{:S(2)}, u32[]{:S(2)}) async-start(bf16[64,8,2048]{2,1,0:T(8,128)(2,1)} %all-reduce.2.cloned.1.call-done), calls=%async_computation.2 | async-start | bytes 4194304 | tf_op jit(solution)/shard_map/all_to_all | solution.py:73
  266.1 1.4 fusion.4
  267.5 0.0 copy-start.3
  267.5 0.0 copy-start.4
  267.5 1.4 fusion.3
  268.9 0.0 copy-done.3
  268.9 0.0 copy-done.4
  268.9 3.0 fusion.5
  271.9 52.2 %all-to-all-done.2 = bf16[64,8,2048]{2,1,0:T(8,128)(2,1)} async-done(((bf16[64,8,2048]{2,1,0:T(8,128)(2,1)}), bf16[64,8,2048]{2,1,0:T(8,128)(2,1)}, u32[]{:S(2)}, u32[]{:S(2)}) %all-to-all-start.2) | async-done | bytes 2097184 | tf_op jit(solution)/shard_map/all_to_all | solution.py:73
  324.1 2.0 convolution_convert_fusion.5
  (2 shorter events, 0.0 us)
Async XLA Ops:
  7.2 112.7 %copy-start = (bf16[1,176,2048]{2,1,0:T(8,128)(2,1)S(1)}, bf16[1,176,2048]{2,1,0:T(8,128)(2,1)}, u32[]{:S(2)}) copy-start(bf16[1,176,2048]{2,1,0:T(8,128)(2,1)} %param.9) | copy-start | bytes 2162692
  7.2 35.8 %all-gather.5.cloned.1.call-start = ((), (), s32[]{:S(2)}) async-start(), calls=%async_computation.4 | async-start | bytes 1179648 | tf_op jit(solution)/shard_map/all_gather | solution.py:30
  46.3 63.8 %all-to-all-start.1 = ((bf16[64,8,2048]{2,1,0:T(8,128)(2,1)}), bf16[64,8,2048]{2,1,0:T(8,128)(2,1)S(1)}, u32[]{:S(2)}, u32[]{:S(2)}) async-start(bf16[64,8,2048]{2,1,0:T(8,128)(2,1)} %fusion.1), calls=%async_computation.1 | async-start | bytes 4194304 | tf_op jit(solution)/shard_map/all_to_all | solution.py:34
  59.1 32.5 %all-gather.3.cloned.1.call-start = ((), (), s32[]{:S(2)}) async-start(), calls=%async_computation.3 | async-start | bytes 1179648 | tf_op jit(solution)/shard_map/all_gather | solution.py:31
  110.1 59.9 %all-to-all-start = ((bf16[64,8,2048]{2,1,0:T(8,128)(2,1)}), bf16[64,8,2048]{2,1,0:T(8,128)(2,1)}, u32[]{:S(2)}, u32[]{:S(2)}) async-start(bf16[64,8,2048]{2,1,0:T(8,128)(2,1)} %fusion), calls=%async_computation | async-start | bytes 4194304 | tf_op jit(solution)/shard_map/all_to_all | solution.py:35
  119.8 1.7 copy-start.1
  119.8 133.3 %all-reduce.2.cloned.1.call-start = ((), (), s32[]{:S(2)}) async-start(), calls=%async_computation.5 | async-start | bytes 4194304 | tf_op jit(solution)/shard_map/psum | solution.py:72
  172.8 1.1 copy-start.2
  253.1 71.1 %all-to-all-start.2 = ((bf16[64,8,2048]{2,1,0:T(8,128)(2,1)}), bf16[64,8,2048]{2,1,0:T(8,128)(2,1)}, u32[]{:S(2)}, u32[]{:S(2)}) async-start(bf16[64,8,2048]{2,1,0:T(8,128)(2,1)} %all-reduce.2.cloned.1.call-done), calls=%async_computation.2 | async-start | bytes 4194304 | tf_op jit(solution)/shard_map/all_to_all | solution.py:73
  267.5 1.4 copy-start.3
  267.5 1.4 copy-start.4
Sparse Core Ops, SparseCore 0:
  10.1 32.8 all-gather.4
  62.0 29.4 all-gather.2
  176.2 76.8 all-reduce.1
where the time goes:
time: 333 us
  waiting for transfers between devices  257 us (77%)
  starting transfers between devices  35.7 us (11%)
  matrix products  23.2 us (7%)
  between operations  13.8 us (4%)
    psum x1, waiting for transfers between devices, on_device(): totals = lax.psum(partial_rows.astype(jnp.bfloat16), 'tensor')  77 us
    all_to_all x1, waiting for transfers between devices, on_device(): lax.all_to_all(totals.reshape(experts, capacity, full_width), 'expert', s...  52.2 us
    all_to_all x1, waiting for transfers between devices, on_device(): lax.all_to_all(spread(full_dy), 'expert', split_axis=0, concat_axis=0, ti...  46.9 us
    all_gather x1, waiting for transfers between devices, on_device(): lax.all_gather(tokens, 'tensor', axis=1, tiled=True)  32.1 us
    all_gather x1, waiting for transfers between devices, on_device(): lax.all_gather(upstream, 'tensor', axis=1, tiled=True)  31.7 us
    all_to_all x1, waiting for transfers between devices, on_device(): lax.all_to_all(spread(full_x), 'expert', split_axis=0, concat_axis=0, til...  15.2 us
    all_to_all x1, starting transfers between devices, on_device(): lax.all_to_all(totals.reshape(experts, capacity, full_width), 'expert', s...  13 us
    all_to_all x1, starting transfers between devices, on_device(): lax.all_to_all(spread(full_x), 'expert', split_axis=0, concat_axis=0, til...  12.8 us
  transfers between devices with their start and end apart: 6, of which 6 were waited for; matrix products, arithmetic and copies ran while one was open for 5% of the time, Pallas kernels for 0%

commit v1 on v0

--- a/solution.py
+++ b/solution.py
@@ -20,22 +20,15 @@
     gate_rows = w_gate[0]
     up_rows = w_up[0]
     down_rows = w_down[0]
-    full_width = gate_rows.shape[1]
 
-    def spread(values):
-        placed = jnp.dot(placing, values, preferred_element_type=jnp.float32).astype(jnp.bfloat16)
-        return placed.reshape(experts, capacity, values.shape[1])
-
-    full_x, full_dy = (
-        lax.all_gather(tokens, "tensor", axis=1, tiled=True),
-        lax.all_gather(upstream, "tensor", axis=1, tiled=True),
-    )
-    got_x, got_dy = (
-        lax.all_to_all(spread(full_x), "expert", split_axis=0, concat_axis=0, tiled=True),
-        lax.all_to_all(spread(full_dy), "expert", split_axis=0, concat_axis=0, tiled=True),
-    )
-    x_all = got_x.reshape(slot_count, full_width)
-    dy_all = got_dy.reshape(slot_count, full_width)
+    feat = tokens.shape[1]
+    own = jnp.concatenate([tokens, upstream], axis=1)
+    placed = jnp.dot(placing, own, preferred_element_type=jnp.float32).astype(jnp.bfloat16)
+    got = lax.all_to_all(
+        placed.reshape(experts, capacity, 2 * feat), "expert", split_axis=0, concat_axis=0, tiled=True
+    ).reshape(slot_count, 2 * feat)
+    x_all = lax.all_gather(got[:, :feat], "tensor", axis=1, tiled=True)
+    dy_all = lax.all_gather(got[:, feat:], "tensor", axis=1, tiled=True)
     gate_pre = lax.dot_general(
         x_all, gate_rows, (((1,), (1,)), ((), ())), preferred_element_type=jnp.float32
     )
@@ -68,21 +61,12 @@
     partial_rows = jnp.dot(d_gate, gate_rows, preferred_element_type=jnp.float32) + jnp.dot(
         d_up, up_rows, preferred_element_type=jnp.float32
     )
-    feat_width = tokens.shape[1]
-    totals = lax.psum(partial_rows.astype(jnp.bfloat16), "tensor")
-    arrived = lax.all_to_all(
-        totals.reshape(experts, capacity, full_width),
-        "expert",
-        split_axis=0,
-        concat_axis=0,
-        tiled=True,
+    totals = lax.psum_scatter(
+        partial_rows.astype(jnp.bfloat16), "tensor", scatter_dimension=1, tiled=True
     )
-    returned = lax.dynamic_slice_in_dim(
-        arrived.reshape(slot_count, full_width),
-        lax.axis_index("tensor") * feat_width,
-        feat_width,
-        1,
-    )
+    returned = lax.all_to_all(
+        totals.reshape(experts, capacity, feat), "expert", split_axis=0, concat_axis=0, tiled=True
+    ).reshape(slot_count, feat)
     grad_tokens = lax.dot_general(
         placing, returned, (((0,), (0,)), ((), ())), preferred_element_type=jnp.float32
     ).astype(jnp.bfloat16)

time: 333 us -> 190 us (0.57)
  the two profiles are of different devices: /device:TPU:15 before, /device:TPU:8 now
where the time goes in v1:
time: 190 us
  waiting for transfers between devices  105 us (55%)
  blocking collectives  35.8 us (19%)
  matrix products  17.1 us (9%)
  between operations  13.8 us (7%)
  starting transfers between devices  13.5 us (7%)
  other arithmetic  2.86 us (2%)
  local copies, waits for them, and re-layouts  1.96 us (1%)
    reduce_scatter x1, waiting for transfers between devices, on_device(): lax.psum_scatter(partial_rows.astype(jnp.bfloat16), 'tensor', scatter_dim...  40.3 us
    all_to_all x1, blocking collectives, on_device(): lax.all_to_all(placed.reshape(experts, capacity, 2 * feat), 'expert', spl...  35.8 us
    all_gather x1, waiting for transfers between devices, on_device(): dy_all = lax.all_gather(got[:, feat:], 'tensor', axis=1, tiled=True)  30.9 us
    all_gather x1, waiting for transfers between devices, on_device(): x_all = lax.all_gather(got[:, :feat], 'tensor', axis=1, tiled=True)  24.7 us
    all_to_all x1, starting transfers between devices, on_device(): lax.all_to_all(totals.reshape(experts, capacity, feat), 'expert', split_a...  13.4 us
    all_to_all x1, waiting for transfers between devices, on_device(): lax.all_to_all(totals.reshape(experts, capacity, feat), 'expert', split_a...  8.21 us
  transfers between devices with their start and end apart: 4, of which 4 were waited for; matrix products, arithmetic and copies ran while one was open for 5% of the time, Pallas kernels for 0%

profile of v1, /device:TPU:8, one launch (start us, length us, event | category | flops | bytes accessed | tf_op | source)
XLA Modules:
  0.0 189.8 jit_solution(1138605556220247862)
XLA Ops:
  7.2 0.0 copy-start
  7.2 0.0 all-gather.5.cloned.1.call-start
  7.2 0.7 fusion.23
  8.0 0.6 reduce-window.6
  8.6 0.2 slice_reduce_fusion
  8.8 0.8 fusion.22
  9.6 0.7 multiply_add_fusion
  10.3 1.3 fusion.3
  11.6 35.8 %all_to_all.10 = bf16[64,8,512]{2,1,0:T(8,128)(2,1)S(1)} all-to-all(bf16[64,8,512]{2,1,0:T(8,128)(2,1)S(1)} %fusion.3), channel_id=1, replica_groups=mesh['expert'=64,'tensor'=8] {'expert'}, dimensions={0} | all-to-all | bytes 1048576 | tf_op jit(solution)/shard_map/all_to_all | solution.py:27
  47.3 0.8 fusion.27
  48.2 0.0 all-gather.5.cloned.1.call-update
  48.2 0.0 all-gather.3.cloned.1.call-start
  48.2 0.7 all-gather.3.cloned.1.call-update
  48.9 0.0 copy-start.2
  48.9 0.0 reduce-scatter.2.cloned.1.call-start
  49.0 24.7 %all-gather.5.cloned.1.call-done = bf16[512,2048]{1,0:T(8,128)(2,1)} async-done(((bf16[512,256]{1,0:T(8,128)(2,1)}), bf16[512,2048]{1,0:T(8,128)(2,1)}) %all-gather.5.cloned.1.call-update) | async-done | bytes 2097168 | tf_op jit(solution)/shard_map/all_gather | solution.py:30
  73.7 0.0 copy-done
  73.7 0.0 copy-start.1
  73.7 3.3 %fusion.6 = f32[512,176]{0,1:T(8,128)} fusion(bf16[512,2048]{1,0:T(8,128)(2,1)} %all-gather.5.cloned.1.call-done, bf16[1,176,2048]{2,1,0:T(8,128)(2,1)S(1)} %copy-done), kind=kOutput, calls=%fused_computation.12 | convolution fusion | flops 369098752 | bytes 3178496 | tf_op jit(solution)/shard_map/dot_general | solution.py:32
  77.1 0.0 copy-done.2
  77.1 0.0 copy-done.1
  77.1 1.6 fusion.9
  78.6 30.9 %all-gather.3.cloned.1.call-done = bf16[512,2048]{1,0:T(8,128)(2,1)} async-done(((bf16[512,256]{1,0:T(8,128)(2,1)}), bf16[512,2048]{1,0:T(8,128)(2,1)}) %all-gather.3.cloned.1.call-update) | async-done | bytes 2097168 | tf_op jit(solution)/shard_map/all_gather | solution.py:31
  109.5 2.8 %multiply_convert_fusion.1 = (bf16[512,176]{0,1:T(8,128)(2,1)S(1)}, bf16[512,176]{0,1:T(8,128)(2,1)S(1)}) fusion(f32[512,176]{0,1:T(8,128)} %fusion.6, f32[512,176]{0,1:T(8,128)} %fusion.9, bf16[512,2048]{1,0:T(8,128)(2,1)} %all-gather.3.cloned.1.call-done, bf16[1,176,2048]{2,1,0:T(8,128)(2,1)} %param.11), kind=kOutput, calls=%fused_computation.21 | convolution fusion | flops 370270208 | bytes 3899392 | tf_op jit(solution)/shard_map/dot_general | solution.py:42
  112.4 0.0 copy-start.3
  112.4 0.8 fusion.4
  113.1 0.4 copy-done.3
  113.5 2.1 %add_convert_fusion = bf16[512,2048]{1,0:T(8,128)(2,1)} fusion(f32[512,2048]{1,0:T(8,128)S(1)} %fusion.4, bf16[512,176]{0,1:T(8,128)(2,1)S(1)} %get-tuple-element.4, bf16[1,176,2048]{2,1,0:T(8,128)(2,1)S(1)} %copy-done.3), kind=kOutput, calls=%fused_computation | convolution fusion | flops 371195904 | bytes 7192576 | tf_op jit(solution)/shard_map/dot_general | solution.py:61
  115.5 0.0 reduce-scatter.2.cloned.1.call-update
  115.6 40.3 %reduce-scatter.2.cloned.1.call-done = bf16[512,256]{1,0:T(8,128)(2,1)} async-done(((bf16[512,2048]{1,0:T(8,128)(2,1)}), bf16[512,256]{1,0:T(8,128)(2,1)}) %reduce-scatter.2.cloned.1.call-update) | async-done | bytes 262160 | tf_op jit(solution)/shard_map/reduce_scatter | solution.py:64
  155.9 13.4 %all-to-all-start.1 = ((bf16[64,8,256]{2,1,0:T(8,128)(2,1)}), bf16[64,8,256]{2,1,0:T(8,128)(2,1)S(1)}, u32[]{:S(2)}, u32[]{:S(2)}) async-start(bf16[64,8,256]{2,1,0:T(8,128)(2,1)} %bitcast.60), calls=%async_computation.2 | async-start | bytes 524288 | tf_op jit(solution)/shard_map/all_to_all | solution.py:67
  169.2 1.4 fusion.1
  170.7 0.0 copy-start.4
  170.7 0.0 copy-start.5
  170.7 0.0 copy-start.6
  170.7 1.4 fusion
  172.1 0.3 copy-done.4
  172.4 0.1 copy-done.5
  172.5 0.1 copy-done.6
  172.6 1.4 fusion.2
  174.1 8.2 %all-to-all-done.1 = bf16[64,8,256]{2,1,0:T(8,128)(2,1)S(1)} async-done(((bf16[64,8,256]{2,1,0:T(8,128)(2,1)}), bf16[64,8,256]{2,1,0:T(8,128)(2,1)S(1)}, u32[]{:S(2)}, u32[]{:S(2)}) %all-to-all-start.1) | async-done | bytes 262176 | tf_op jit(solution)/shard_map/all_to_all | solution.py:67
  182.3 1.0 convolution_convert_fusion.4
  (2 shorter events, 0.0 us)
Async XLA Ops:
  7.2 66.6 %copy-start = (bf16[1,176,2048]{2,1,0:T(8,128)(2,1)S(1)}, bf16[1,176,2048]{2,1,0:T(8,128)(2,1)}, u32[]{:S(2)}) copy-start(bf16[1,176,2048]{2,1,0:T(8,128)(2,1)} %param.9) | copy-start | bytes 2162692
  7.2 66.5 %all-gather.5.cloned.1.call-start = ((), (), s32[]{:S(2)}) async-start(), calls=%async_computation.4 | async-start | bytes 2359296 | tf_op jit(solution)/shard_map/all_gather | solution.py:30
  48.2 61.4 %all-gather.3.cloned.1.call-start = ((), (), s32[]{:S(2)}) async-start(), calls=%async_computation.3 | async-start | bytes 2359296 | tf_op jit(solution)/shard_map/all_gather | solution.py:31
  48.9 28.1 %copy-start.2 = (bf16[1,176,2048]{2,1,0:T(8,128)(2,1)S(1)}, bf16[1,176,2048]{2,1,0:T(8,128)(2,1)}, u32[]{:S(2)}) copy-start(bf16[1,176,2048]{2,1,0:T(8,128)(2,1)} %param.10) | copy-start | bytes 2162692
  48.9 106.9 %reduce-scatter.2.cloned.1.call-start = ((), (), s32[]{:S(2)}) async-start(), calls=%async_computation.5 | async-start | bytes 2359296 | tf_op jit(solution)/shard_map/reduce_scatter | solution.py:64
  73.7 3.3 %copy-start.1 = (bf16[512,2048]{1,0:T(8,128)(2,1)S(1)}, bf16[512,2048]{1,0:T(8,128)(2,1)}, u32[]{:S(2)}) copy-start(bf16[512,2048]{1,0:T(8,128)(2,1)} %all-gather.5.cloned.1.call-done) | copy-start | bytes 6291460
  112.4 1.1 copy-start.3
  155.9 26.4 %all-to-all-start.1 = ((bf16[64,8,256]{2,1,0:T(8,128)(2,1)}), bf16[64,8,256]{2,1,0:T(8,128)(2,1)S(1)}, u32[]{:S(2)}, u32[]{:S(2)}) async-start(bf16[64,8,256]{2,1,0:T(8,128)(2,1)} %bitcast.60), calls=%async_computation.2 | async-start | bytes 524288 | tf_op jit(solution)/shard_map/all_to_all | solution.py:67
  170.7 1.7 copy-start.4
  170.7 1.9 copy-start.5
  170.7 2.0 %copy-start.6 = (f32[512,176]{0,1:T(8,128)S(1)}, f32[512,176]{0,1:T(8,128)}, u32[]{:S(2)}) copy-start(f32[512,176]{0,1:T(8,128)} %fusion.9) | copy-start | bytes 1081348
Sparse Core Ops, SparseCore 0:
  48.3 25.3 all-gather.4
  76.4 33.0 all-gather.2
  115.7 40.1 reduce-scatter.1

commit v2 on v1

v2 whole, which is shorter than its diff:
```python
import functools

import jax
import jax.numpy as jnp
from jax import lax
from jax.experimental import pallas as pl
from jax.experimental.pallas import tpu as pltpu
from jax.sharding import PartitionSpec as P

MESH = pl.DeviceIdType.MESH
F32 = jnp.float32
BF16 = jnp.bfloat16
CAP = 8
Y_SIDE = 8
CHUNKS = 4


def log2(value):
    return value.bit_length() - 1


def offset_of(place):
    odd = lax.rem(place, 2)
    return lax.div(place + 1, 2) * (2 * odd - 1)


def place_of(distance, side):
    return jnp.where(
        distance <= side // 2, jnp.maximum(2 * distance - 1, 0), 2 * (side - distance)
    )


def kernel(
    sizes,
    tok_ref,
    up_ref,
    ids_ref,
    wg_hbm,
    wu_hbm,
    wd_hbm,
    gt_ref,
    gg_ref,
    gu_ref,
    gd_ref,
    send,
    recv,
    gath,
    weights,
    grads,
    acts,
    part,
    sib_out,
    sib_in,
    half_out,
    half_in,
    full_out,
    full_in,
    ret_out,
    ret_in,
    w_sem,
    a2a_s,
    a2a_r,
    ag_s,
    ag_r,
    rs_s,
    rs_r,
    ret_s,
    ret_r,
    out_sem,
):
    zs, ys, xs, chunks = sizes
    experts = zs * ys
    rows_all = experts * CAP
    tok_rows, feat = tok_ref.shape
    blocks = experts // chunks
    rows = blocks * CAP
    half = rows // 2
    planes = zs // chunks
    hid = weights.shape[1]
    iters = chunks + 6

    e = lax.axis_index("expert")
    t = lax.axis_index("tensor")
    z, y = lax.div(e, ys), lax.rem(e, ys)
    x, c = lax.div(t, 2), lax.rem(t, 2)
    own = 2 * x + c
    right_x, left_x, far_x = lax.rem(x + 1, xs), lax.rem(x + xs - 1, xs), lax.rem(x + 2, xs)
    right, left, sib = (e, 2 * right_x + c), (e, 2 * left_x + c), (e, 2 * x + 1 - c)

    def peer(r, sign):
        dz, dy = offset_of(lax.div(r, ys)), offset_of(lax.rem(r, ys))
        pz, py = lax.rem(z + sign * dz + zs, zs), lax.rem(y + sign * dy + ys, ys)
        return (pz * ys + py, t)

    def remote(src, dst, ssem, rsem, device):
        return pltpu.make_async_remote_copy(
            src_ref=src,
            dst_ref=dst,
            send_sem=ssem,
            recv_sem=rsem,
            device_id=device,
            device_id_type=MESH,
        )

    barrier = pltpu.get_barrier_semaphore()

    def greet(r, carry):
        pl.semaphore_signal(barrier, inc=1, device_id=peer(r, 1), device_id_type=MESH)
        return carry

    for near in (right, left, sib):
        pl.semaphore_signal(barrier, inc=1, device_id=near, device_id_type=MESH)
    lax.fori_loop(1, experts, greet, 0)

    fetches = [
        pltpu.make_async_copy(w.at[0], weights.at[m], w_sem.at[m])
        for m, w in enumerate((wg_hbm, wu_hbm, wd_hbm))
    ]
    for fetch in fetches:
        fetch.start()

    ids = ids_ref[...]
    dz = (lax.shift_right_logical(ids, log2(ys)) - z) & (zs - 1)
    dy = ((ids & (ys - 1)) - y) & (ys - 1)
    rel = place_of(dz, zs) * ys + place_of(dy, ys)
    onehot = jnp.where(rel == lax.broadcasted_iota(jnp.int32, (tok_rows, experts), 1), 1.0, 0.0)
    row_i = lax.broadcasted_iota(jnp.int32, (tok_rows, tok_rows), 0)
    col_i = lax.broadcasted_iota(jnp.int32, (tok_rows, tok_rows), 1)
    earlier = jnp.where(col_i < row_i, 1.0, 0.0).astype(BF16)
    before = jnp.dot(earlier, onehot.astype(BF16), preferred_element_type=F32)
    within = jnp.sum(before * onehot, axis=1, keepdims=True)
    slot = rel.astype(F32) * float(CAP) + within
    slot_row = jnp.sum(jnp.where(row_i == col_i, slot, 0.0), axis=0, keepdims=True)
    slot_row = slot_row.astype(jnp.int32)
    slot_col = slot.astype(jnp.int32)
    placing = jnp.where(
        lax.broadcasted_iota(jnp.int32, (rows_all, tok_rows), 0) == slot_row, 1.0, 0.0
    ).astype(BF16)
    placed_x = jnp.dot(placing, tok_ref[...], preferred_element_type=F32)
    placed_d = jnp.dot(placing, up_ref[...], preferred_element_type=F32)
    send[:, 0:CAP, :] = placed_x.reshape(experts, CAP, feat).astype(BF16)
    send[:, CAP : 2 * CAP, :] = placed_d.reshape(experts, CAP, feat).astype(BF16)

    pl.semaphore_wait(barrier, experts - 1 + 3)

    def dispatch(r, carry):
        remote(
            send.at[r], recv.at[r], a2a_s, a2a_r.at[lax.div(r, blocks)], peer(r, 1)
        ).start()
        return carry

    pltpu.make_async_copy(send.at[0], recv.at[0], a2a_r.at[0]).start()
    lax.fori_loop(1, experts, dispatch, 0)

    def span(j):
        return pl.ds(pl.multiple_of(j * rows, rows), rows)

    def gather_copy(kind, j):
        s = span(j)
        left_b, right_b, far_b = 2 * left_x + c, 2 * right_x + c, 2 * far_x + c
        at, device = {
            0: (gath.at[own, :, s], right),
            1: (gath.at[own, :, s], left),
            2: (gath.at[left_b, 0, s], right),
            3: (gath.at[right_b, 1, s], left),
            4: (gath.at[own, :, s], sib),
            5: (gath.at[left_b, :, s], sib),
            6: (gath.at[right_b, :, s], sib),
            7: (gath.at[far_b, :, s], sib),
        }[kind]
        return remote(at, at, ag_s.at[kind, j], ag_r.at[kind, j], device)

    def gather_wait(kind, j):
        s = span(j)
        left_b, right_b, far_b = 2 * left_x + c, 2 * right_x + c, 2 * far_x + c
        o = 1 - 2 * c
        at, device = {
            0: (gath.at[left_b, :, s], right),
            1: (gath.at[right_b, :, s], left),
            2: (gath.at[far_b, 0, s], right),
            3: (gath.at[far_b, 1, s], left),
            4: (gath.at[own + o, :, s], sib),
            5: (gath.at[left_b + o, :, s], sib),
            6: (gath.at[right_b + o, :, s], sib),
            7: (gath.at[far_b + o, :, s], sib),
        }[kind]
        remote(at, at, ag_s.at[kind, j], ag_r.at[kind, j], device).wait_recv()

    def sum_copy(kind, j):
        src, dst, device = {
            0: (sib_out.at[j], sib_in.at[j], sib),
            1: (half_out.at[j, 0], half_in.at[j, 0], right),
            2: (half_out.at[j, 1], half_in.at[j, 1], left),
            3: (full_out.at[j, 0], full_in.at[j, 0], right),
            4: (full_out.at[j, 1], full_in.at[j, 1], left),
        }[kind]
        return remote(src, dst, rs_s.at[kind, j], rs_r.at[kind, j], device)

    def take_in(j):
        at = recv.at[pl.ds(j * blocks, blocks)]
        remote(at, at, a2a_s, a2a_r.at[j], sib).wait_recv()
        got = recv[pl.ds(j * blocks, blocks)].astype(F32)
        gath[own, 0, span(j), :] = got[:, 0:CAP, :].reshape(rows, feat).astype(BF16)
        gath[own, 1, span(j), :] = got[:, CAP : 2 * CAP, :].reshape(rows, feat).astype(BF16)
        for kind in (0, 1, 4):
            gather_copy(kind, j).start()

    def pass_near(j):
        gather_wait(0, j)
        gather_copy(2, j).start()
        gather_copy(5, j).start()
        gather_wait(1, j)
        gather_copy(3, j).start()
        gather_copy(6, j).start()

    def pass_far(j):
        gather_wait(2, j)
        gather_wait(3, j)
        gather_copy(7, j).start()

    def columns(b):
        return pl.ds(pl.multiple_of(b * feat, feat), feat)

    def multiply(j):
        for kind in (4, 5, 6, 7):
            gather_wait(kind, j)
        contract = (((1,), (1,)), ((), ()))
        gate = jnp.zeros((rows, hid), F32)
        up = jnp.zeros((rows, hid), F32)
        d_hidden = jnp.zeros((rows, hid), F32)
        for b in range(2 * xs):
            xb = gath[b, 0, span(j), :]
            db = gath[b, 1, span(j), :]
            at = slice(b * feat, (b + 1) * feat)
            gate += lax.dot_general(xb, weights[0, :, at], contract, preferred_element_type=F32)
            up += lax.dot_general(xb, weights[1, :, at], contract, preferred_element_type=F32)
            d_hidden += lax.dot_general(db, weights[2, :, at], contract, preferred_element_type=F32)
        sig = jax.nn.sigmoid(gate)
        silu = gate * sig
        hidden = (silu * up).astype(BF16)
        d_up = (d_hidden * silu).astype(BF16)
        d_gate = (d_hidden * up * sig * (1.0 + gate * (1.0 - sig))).astype(BF16)
        acts[0, span(j), :] = d_gate
        acts[1, span(j), :] = d_up
        acts[2, span(j), :] = hidden

        def rows_of(b):
            return jnp.dot(
                d_gate, weights[0, :, columns(b)], preferred_element_type=F32
            ) + jnp.dot(d_up, weights[1, :, columns(b)], preferred_element_type=F32)

        for k in range(xs):
            sib_out[j, k] = rows_of(2 * lax.rem(x + k, xs) + 1 - c).astype(BF16)
        sum_copy(0, j).start()
        for k in range(xs):
            part[j, k] = rows_of(2 * lax.rem(x + k, xs) + c)

    def sum_far(j):
        sum_copy(0, j).wait_recv()
        total = part[j, 2] + sib_in[j, 2].astype(F32)
        half_out[j, 0] = total[0:half].astype(BF16)
        half_out[j, 1] = total[half:rows].astype(BF16)
        sum_copy(1, j).start()
        sum_copy(2, j).start()

    def sum_near(j):
        to_right = part[j, 1] + sib_in[j, 1].astype(F32)
        to_left = part[j, 3] + sib_in[j, 3].astype(F32)
        sum_copy(1, j).wait_recv()
        full_out[j, 0, 0:half] = (to_right[0:half] + half_in[j, 0].astype(F32)).astype(BF16)
        full_out[j, 0, half:rows] = to_right[half:rows].astype(BF16)
        sum_copy(3, j).start()
        sum_copy(2, j).wait_recv()
        full_out[j, 1, 0:half] = to_left[0:half].astype(BF16)
        full_out[j, 1, half:rows] = (to_left[half:rows] + half_in[j, 1].astype(F32)).astype(BF16)
        sum_copy(4, j).start()

    def give_back(j):
        total = part[j, 0] + sib_in[j, 0].astype(F32)
        sum_copy(3, j).wait_recv()
        total += full_in[j, 0].astype(F32)
        sum_copy(4, j).wait_recv()
        total += full_in[j, 1].astype(F32)
        split = total.reshape(blocks, CAP, feat)
        ret_out[pl.ds(j * blocks, blocks), 0:CAP, :] = split[:, :, 0 : feat // 2].astype(BF16)
        ret_out[pl.ds(j * blocks, blocks), CAP : 2 * CAP, :] = split[:, :, feat // 2 :].astype(BF16)

        @pl.when(j == 0)
        def _():
            pltpu.make_async_copy(ret_out.at[0], ret_in.at[0], ret_r).start()

        def back(r, carry):
            remote(ret_out.at[r], ret_in.at[r], ret_s, ret_r, peer(r, -1)).start()
            return carry

        lax.fori_loop(jnp.maximum(j * blocks, 1), (j + 1) * blocks, back, 0)

    def step(i, carry):
        def stage(lag, work):
            @pl.when(jnp.logical_and(i >= lag, i < chunks + lag))
            def _():
                work(i - lag)

        stage(0, take_in)
        stage(1, pass_near)
        stage(2, pass_far)
        stage(6, give_back)
        stage(5, sum_near)
        stage(4, sum_far)

        @pl.when(i == 3)
        def _():
            for fetch in fetches:
                fetch.wait()

        stage(3, multiply)
        return carry

    lax.fori_loop(0, iters, step, 0)

    outs = (gg_ref, gu_ref, gd_ref)
    for m in range(3):
        turned = acts[m].T
        side = 1 if m == 2 else 0

        def column(b, carry):
            grads[m, :, columns(b)] = jnp.dot(
                turned, gath[b, side], preferred_element_type=F32
            ).astype(BF16)
            return carry

        lax.fori_loop(0, 2 * xs, column, 0)
        pltpu.make_async_copy(grads.at[m], outs[m].at[0], out_sem.at[m]).start()

    picking = jnp.where(
        lax.broadcasted_iota(jnp.int32, (tok_rows, rows_all), 1) == slot_col, 1.0, 0.0
    ).astype(BF16)
    remote(ret_in, ret_in, ret_s, ret_r, sib).wait_recv()
    back = ret_in[...].astype(F32)
    low = back[:, 0:CAP, :].reshape(rows_all, feat // 2).astype(BF16)
    high = back[:, CAP : 2 * CAP, :].reshape(rows_all, feat // 2).astype(BF16)
    gt_ref[:, 0 : feat // 2] = jnp.dot(picking, low, preferred_element_type=F32).astype(BF16)
    gt_ref[:, feat // 2 :] = jnp.dot(picking, high, preferred_element_type=F32).astype(BF16)

    rest = send.at[pl.ds(1, experts - 1)]
    remote(rest, rest, a2a_s, a2a_r.at[0], sib).wait_send()
    rest = ret_out.at[pl.ds(1, experts - 1)]
    remote(rest, rest, ret_s, ret_r, sib).wait_send()

    def drain(j, carry):
        for kind in range(8):
            gather_copy(kind, j).wait_send()
        for kind in range(5):
            sum_copy(kind, j).wait_send()
        return carry

    lax.fori_loop(0, chunks, drain, 0)
    for m in range(3):
        pltpu.make_async_copy(grads.at[m], outs[m].at[0], out_sem.at[m]).wait()


def on_device(tokens, upstream, expert_ids, w_gate, w_up, w_down):
    experts = lax.axis_size("expert")
    devices = lax.axis_size("tensor")
    ys = Y_SIDE
    zs, xs, chunks = experts // ys, devices // 2, CHUNKS
    tok_rows, feat = tokens.shape
    hid, width = w_gate.shape[1:]
    slots = experts * CAP
    rows = slots // chunks
    whole = pl.BlockSpec(memory_space=pltpu.VMEM)
    away = pl.BlockSpec(memory_space=pl.ANY)
    dma = pltpu.SemaphoreType.DMA
    return pl.pallas_call(
        functools.partial(kernel, (zs, ys, xs, chunks)),
        out_shape=(
            jax.ShapeDtypeStruct((tok_rows, feat), BF16),
            jax.ShapeDtypeStruct(w_gate.shape, BF16),
            jax.ShapeDtypeStruct(w_up.shape, BF16),
            jax.ShapeDtypeStruct(w_down.shape, BF16),
        ),
        in_specs=[whole, whole, whole, away, away, away],
        out_specs=(whole, away, away, away),
        scratch_shapes=[
            pltpu.VMEM((experts, 2 * CAP, feat), BF16),
            pltpu.VMEM((experts, 2 * CAP, feat), BF16),
            pltpu.VMEM((devices, 2, slots, feat), BF16),
            pltpu.VMEM((3, hid, width), BF16),
            pltpu.VMEM((3, hid, width), BF16),
            pltpu.VMEM((3, slots, hid), BF16),
            pltpu.VMEM((chunks, xs, rows, feat), F32),
            pltpu.VMEM((chunks, xs, rows, feat), BF16),
            pltpu.VMEM((chunks, xs, rows, feat), BF16),
            pltpu.VMEM((chunks, 2, rows // 2, feat), BF16),
            pltpu.VMEM((chunks, 2, rows // 2, feat), BF16),
            pltpu.VMEM((chunks, 2, rows, feat), BF16),
            pltpu.VMEM((chunks, 2, rows, feat), BF16),
            pltpu.VMEM((experts, 2 * CAP, feat // 2), BF16),
            pltpu.VMEM((experts, 2 * CAP, feat // 2), BF16),
            dma((3,)),
            dma,
            dma((chunks,)),
            dma((8, chunks)),
            dma((8, chunks)),
            dma((5, chunks)),
            dma((5, chunks)),
            dma,
            dma,
            dma((3,)),
        ],
        compiler_params=pltpu.CompilerParams(
            collective_id=0, has_side_effects=True, vmem_limit_bytes=48 * 1024 * 1024
        ),
    )(tokens, upstream, expert_ids, w_gate, w_up, w_down)


def solution(mesh):
    in_specs = (
        P("expert", "tensor"),
        P("expert", "tensor"),
        P("expert", None),
        P("expert", "tensor", None),
        P("expert", "tensor", None),
        P("expert", "tensor", None),
    )
    out_specs = (
        P("expert", "tensor"),
        P("expert", "tensor", None),
        P("expert", "tensor", None),
        P("expert", "tensor", None),
    )
    return jax.shard_map(
        on_device, mesh=mesh, in_specs=in_specs, out_specs=out_specs, check_vma=False
    )
```

time: 190 us -> 83.5 us (0.44)
  waiting for transfers between devices: 105 us -> 0 us
  Pallas kernels: 0 us -> 74.2 us
  blocking collectives: 35.8 us -> 0 us
  matrix products: 17.1 us -> 0 us
  starting transfers between devices: 13.5 us -> 0 us
  between operations: 13.8 us -> 0.66 us
  local copies, waits for them, and re-layouts: 1.96 us -> 8.37 us
  other arithmetic: 2.86 us -> 0 us
    pallas_call x0 -> x1, Pallas kernels: none -> 74.2 us  [on_device(): pl.pallas_call(functools.partial(kernel, (zs, ys, xs, chunks)), out_shape...]
    all_gather x2 -> x0, waiting for transfers between devices: 55.6 us -> none  [the longest x1 30.9 us: on_device(): dy_all = lax.all_gather(got[:, feat:], 'tensor', axis=1, tiled=True)]
    reduce_scatter x1 -> x0, waiting for transfers between devices: 40.3 us -> none  [on_device(): lax.psum_scatter(partial_rows.astype(jnp.bfloat16), 'tensor', scatter_dim...]
    all_to_all x1 -> x0, blocking collectives: 35.8 us -> none  [on_device(): lax.all_to_all(placed.reshape(experts, capacity, 2 * feat), 'expert', spl...]
    dot_general x10 -> x0, matrix products: 17.1 us -> none  [the longest x1 3.33 us: on_device(): lax.dot_general(x_all, gate_rows, (((1,), (1,)), ((), ())), preferred_ele...]
    all_to_all x1 -> x0, starting transfers between devices: 13.4 us -> none  [on_device(): lax.all_to_all(totals.reshape(experts, capacity, feat), 'expert', split_a...]
    all_to_all x1 -> x0, waiting for transfers between devices: 8.21 us -> none  [on_device(): lax.all_to_all(totals.reshape(experts, capacity, feat), 'expert', split_a...]
    unnamed x14 -> x15, local copies, waits for them, and re-layouts: 0.95 us -> 8.37 us
  transfers between devices with their start and end apart: 4 -> 0, of which waited for: 4 -> 0; matrix products, arithmetic and copies ran while one was open for 5% -> 0% of each run, Pallas kernels for 0% -> 0%
where the time goes in v2:
time: 83.5 us; the launch traced here: 83.2 us
  Pallas kernels  74.2 us (89%)
  local copies, waits for them, and re-layouts  8.37 us (10%)
    pallas_call x1, Pallas kernels, on_device(): pl.pallas_call(functools.partial(kernel, (zs, ys, xs, chunks)), out_shape...  74.2 us
    unnamed x15, local copies, waits for them, and re-layouts  8.37 us

profile of v2, /device:TPU:8, one launch (start us, length us, event | category | flops | bytes accessed | tf_op | source)
XLA Modules:
  0.0 83.2 jit_solution(9851433176390379091)
XLA Ops:
  0.6 0.0 copy-start.3
  0.6 0.8 %copy.10.ids_ref = s32[256,1]{1,0:T(8,128)S(1)} copy(s32[256,1]{0,1:T(1,128)} %param.8) | data formatting | bytes 2048 | tf_op args[2]
  1.5 0.1 copy-done.3
  1.6 0.0 copy-start
  1.6 1.1 %copy-done = bf16[1,176,2048]{2,1,0:T(8,128)(2,1)S(1)} copy-done((bf16[1,176,2048]{2,1,0:T(8,128)(2,1)S(1)}, bf16[1,176,2048]{2,1,0:T(8,128)(2,1)}, u32[]{:S(2)}) %copy-start) | copy-done | bytes 720920
  2.7 0.0 copy-start.1
  2.7 1.1 %copy-done.1 = bf16[1,176,2048]{2,1,0:T(8,128)(2,1)S(1)} copy-done((bf16[1,176,2048]{2,1,0:T(8,128)(2,1)S(1)}, bf16[1,176,2048]{2,1,0:T(8,128)(2,1)}, u32[]{:S(2)}) %copy-start.1) | copy-done | bytes 720920
  3.8 0.0 copy-start.2
  3.8 1.1 %copy-done.2 = bf16[1,176,2048]{2,1,0:T(8,128)(2,1)S(1)} copy-done((bf16[1,176,2048]{2,1,0:T(8,128)(2,1)S(1)}, bf16[1,176,2048]{2,1,0:T(8,128)(2,1)}, u32[]{:S(2)}) %copy-start.2) | copy-done | bytes 720920
  4.9 0.0 copy-start.4
  4.9 0.9 %copy-done.4 = bf16[256,256]{1,0:T(8,128)(2,1)S(1)} copy-done((bf16[256,256]{1,0:T(8,128)(2,1)S(1)}, bf16[256,256]{1,0:T(8,128)(2,1)}, u32[]{:S(2)}) %copy-start.4) | copy-done | bytes 131096
  5.8 74.2 %shard_map.93 = (bf16[256,256]{1,0:T(8,128)(2,1)S(1)}, bf16[1,176,2048]{2,1,0:T(8,128)(2,1)S(1)}, bf16[1,176,2048]{2,1,0:T(8,128)(2,1)S(1)}, bf16[1,176,2048]{2,1,0:T(8,128)(2,1)S(1)}) custom-call(bf16[256,256]{1,0:T(8,128)(2,1)S(1)} %copy-done.3, bf16[256,256]{1,0:T(8,128)(2,1)S(1)} %copy-done.4, s32[256,1]{1,0:T(8,128)S(1)} %copy.10.ids_ref, ...), custom_call_target="tpu_custom_call" | custom-call | tf_op jit(solution)/shard_map/pallas_call | solution.py:374
  80.0 0.7 copy.15
  80.6 0.9 %copy.16 = bf16[1,176,2048]{2,1,0:T(8,128)(2,1)} copy(bf16[1,176,2048]{2,1,0:T(8,128)(2,1)S(1)} %get-tuple-element.9) | data formatting | bytes 1441792
  81.5 0.9 %copy.17 = bf16[1,176,2048]{2,1,0:T(8,128)(2,1)} copy(bf16[1,176,2048]{2,1,0:T(8,128)(2,1)S(1)} %get-tuple-element.10) | data formatting | bytes 1441792
  82.3 0.9 %copy.18 = bf16[1,176,2048]{2,1,0:T(8,128)(2,1)} copy(bf16[1,176,2048]{2,1,0:T(8,128)(2,1)S(1)} %get-tuple-element.11) | data formatting | bytes 1441792
Async XLA Ops:
  0.6 0.9 %copy-start.3 = (bf16[256,256]{1,0:T(8,128)(2,1)S(1)}, bf16[256,256]{1,0:T(8,128)(2,1)}, u32[]{:S(2)}) copy-start(bf16[256,256]{1,0:T(8,128)(2,1)} %tok_ref.1) | copy-start | bytes 393220
  1.6 1.1 %copy-start = (bf16[1,176,2048]{2,1,0:T(8,128)(2,1)S(1)}, bf16[1,176,2048]{2,1,0:T(8,128)(2,1)}, u32[]{:S(2)}) copy-start(bf16[1,176,2048]{2,1,0:T(8,128)(2,1)} %wg_hbm.1) | copy-start | bytes 2162692
  2.7 1.1 %copy-start.1 = (bf16[1,176,2048]{2,1,0:T(8,128)(2,1)S(1)}, bf16[1,176,2048]{2,1,0:T(8,128)(2,1)}, u32[]{:S(2)}) copy-start(bf16[1,176,2048]{2,1,0:T(8,128)(2,1)} %wu_hbm.1) | copy-start | bytes 2162692
  3.8 1.1 %copy-start.2 = (bf16[1,176,2048]{2,1,0:T(8,128)(2,1)S(1)}, bf16[1,176,2048]{2,1,0:T(8,128)(2,1)}, u32[]{:S(2)}) copy-start(bf16[1,176,2048]{2,1,0:T(8,128)(2,1)} %wd_hbm.1) | copy-start | bytes 2162692
  4.9 0.9 %copy-start.4 = (bf16[256,256]{1,0:T(8,128)(2,1)S(1)}, bf16[256,256]{1,0:T(8,128)(2,1)}, u32[]{:S(2)}) copy-start(bf16[256,256]{1,0:T(8,128)(2,1)} %up_ref.1) | copy-start | bytes 393220

commit v3 on v2

--- a/solution.py
+++ b/solution.py
@@ -13,28 +13,29 @@
 CAP = 8
 Y_SIDE = 8
 CHUNKS = 4
+LAGS = (0, 1, 2, 3, 4, 5, 6)
 
 
 def log2(value):
     return value.bit_length() - 1
 
 
-def offset_of(place):
-    odd = lax.rem(place, 2)
-    return lax.div(place + 1, 2) * (2 * odd - 1)
-
-
-def place_of(distance, side):
-    return jnp.where(
-        distance <= side // 2, jnp.maximum(2 * distance - 1, 0), 2 * (side - distance)
-    )
+def order_of(zs, ys, count):
+    def far(pair):
+        return min(pair[0], zs - pair[0]) + min(pair[1], ys - pair[1])
+
+    pairs = sorted(((dz, dy) for dz in range(zs) for dy in range(ys)), key=far)
+    ring = [pair for pair in pairs if 0 in pair]
+    pairs = ring + [pair for pair in pairs if 0 not in pair]
+    rest = pairs[count:]
+    return pairs[:count] + rest[:count] + rest[2 * count :] + rest[count : 2 * count]
 
 
 def kernel(
     sizes,
-    tok_ref,
-    up_ref,
-    ids_ref,
+    tok_hbm,
+    up_hbm,
+    ids_hbm,
     wg_hbm,
     wu_hbm,
     wd_hbm,
@@ -42,6 +43,9 @@
     gg_ref,
     gu_ref,
     gd_ref,
+    tok_ref,
+    up_ref,
+    ids_ref,
     send,
     recv,
     gath,
@@ -57,6 +61,8 @@
     full_in,
     ret_out,
     ret_in,
+    torus_sem,
+    in_sem,
     w_sem,
     a2a_s,
     a2a_r,
@@ -75,9 +81,8 @@
     blocks = experts // chunks
     rows = blocks * CAP
     half = rows // 2
-    planes = zs // chunks
     hid = weights.shape[1]
-    iters = chunks + 6
+    iters = chunks + max(LAGS)
 
     e = lax.axis_index("expert")
     t = lax.axis_index("tensor")
@@ -87,10 +92,18 @@
     right_x, left_x, far_x = lax.rem(x + 1, xs), lax.rem(x + xs - 1, xs), lax.rem(x + 2, xs)
     right, left, sib = (e, 2 * right_x + c), (e, 2 * left_x + c), (e, 2 * x + 1 - c)
 
+    order = order_of(zs, ys, blocks)
+
+    def moved(at, offset, side):
+        to = at + offset % side
+        return jnp.where(to >= side, to - side, to)
+
+    to_z = [moved(z, o, zs) * ys for o in range(zs)]
+    to_y = [moved(y, o, ys) for o in range(ys)]
+
     def peer(r, sign):
-        dz, dy = offset_of(lax.div(r, ys)), offset_of(lax.rem(r, ys))
-        pz, py = lax.rem(z + sign * dz + zs, zs), lax.rem(y + sign * dy + ys, ys)
-        return (pz * ys + py, t)
+        dz, dy = order[r]
+        return (to_z[sign * dz % zs] + to_y[sign * dy % ys], t)
 
     def remote(src, dst, ssem, rsem, device):
         return pltpu.make_async_remote_copy(
@@ -104,14 +117,23 @@
 
     barrier = pltpu.get_barrier_semaphore()
 
-    def greet(r, carry):
-        pl.semaphore_signal(barrier, inc=1, device_id=peer(r, 1), device_id_type=MESH)
-        return carry
-
+    for dz in range(1, zs):
+        pl.semaphore_signal(barrier, inc=1, device_id=(to_z[dz] + y, t), device_id_type=MESH)
+    for dy in range(1, ys):
+        pl.semaphore_signal(barrier, inc=1, device_id=(z * ys + to_y[dy], t), device_id_type=MESH)
+    early = [pair for pair in order[:blocks] if 0 not in pair]
+    for dz, dy in early:
+        device = (to_z[-dz % zs] + to_y[-dy % ys], t)
+        pl.semaphore_signal(barrier, inc=1, device_id=device, device_id_type=MESH)
     for near in (right, left, sib):
         pl.semaphore_signal(barrier, inc=1, device_id=near, device_id_type=MESH)
-    lax.fori_loop(1, experts, greet, 0)
-
+
+    loads = [
+        pltpu.make_async_copy(src, dst, in_sem.at[m])
+        for m, (src, dst) in enumerate(((ids_hbm, ids_ref), (tok_hbm, tok_ref), (up_hbm, up_ref)))
+    ]
+    for load in loads:
+        load.start()
     fetches = [
         pltpu.make_async_copy(w.at[0], weights.at[m], w_sem.at[m])
         for m, w in enumerate((wg_hbm, wu_hbm, wd_hbm))
@@ -119,38 +141,44 @@
     for fetch in fetches:
         fetch.start()
 
+    expert_i = lax.broadcasted_iota(jnp.int32, (experts, 1), 0)
+    place = sum(
+        jnp.where(expert_i == dz * ys + dy, CAP * r, 0) for r, (dz, dy) in enumerate(order)
+    ).astype(F32)
+    row_i = lax.broadcasted_iota(jnp.int32, (tok_rows, tok_rows), 0)
+    col_i = lax.broadcasted_iota(jnp.int32, (tok_rows, tok_rows), 1)
+    earlier = jnp.where(row_i < col_i, 1.0, 0.0).astype(BF16)
+    loads[0].wait()
     ids = ids_ref[...]
     dz = (lax.shift_right_logical(ids, log2(ys)) - z) & (zs - 1)
     dy = ((ids & (ys - 1)) - y) & (ys - 1)
-    rel = place_of(dz, zs) * ys + place_of(dy, ys)
-    onehot = jnp.where(rel == lax.broadcasted_iota(jnp.int32, (tok_rows, experts), 1), 1.0, 0.0)
-    row_i = lax.broadcasted_iota(jnp.int32, (tok_rows, tok_rows), 0)
-    col_i = lax.broadcasted_iota(jnp.int32, (tok_rows, tok_rows), 1)
-    earlier = jnp.where(col_i < row_i, 1.0, 0.0).astype(BF16)
-    before = jnp.dot(earlier, onehot.astype(BF16), preferred_element_type=F32)
-    within = jnp.sum(before * onehot, axis=1, keepdims=True)
-    slot = rel.astype(F32) * float(CAP) + within
-    slot_row = jnp.sum(jnp.where(row_i == col_i, slot, 0.0), axis=0, keepdims=True)
-    slot_row = slot_row.astype(jnp.int32)
-    slot_col = slot.astype(jnp.int32)
+    onehot = jnp.where(
+        dz * ys + dy == lax.broadcasted_iota(jnp.int32, (experts, tok_rows), 0), 1.0, 0.0
+    )
+    before = jnp.dot(onehot.astype(BF16), earlier, preferred_element_type=F32)
+    slot = jnp.sum(onehot * (before + place), axis=0, keepdims=True)
+    slot_row = slot.astype(jnp.int32)
+
+    pl.semaphore_wait(barrier, zs + ys - 2 + len(early) + 3)
+    for dz in range(1, zs):
+        pl.semaphore_signal(torus_sem, inc=1, device_id=(to_z[dz] + y, t), device_id_type=MESH)
+
     placing = jnp.where(
         lax.broadcasted_iota(jnp.int32, (rows_all, tok_rows), 0) == slot_row, 1.0, 0.0
     ).astype(BF16)
+    loads[1].wait()
+    loads[2].wait()
     placed_x = jnp.dot(placing, tok_ref[...], preferred_element_type=F32)
     placed_d = jnp.dot(placing, up_ref[...], preferred_element_type=F32)
     send[:, 0:CAP, :] = placed_x.reshape(experts, CAP, feat).astype(BF16)
     send[:, CAP : 2 * CAP, :] = placed_d.reshape(experts, CAP, feat).astype(BF16)
 
-    pl.semaphore_wait(barrier, experts - 1 + 3)
-
-    def dispatch(r, carry):
-        remote(
-            send.at[r], recv.at[r], a2a_s, a2a_r.at[lax.div(r, blocks)], peer(r, 1)
-        ).start()
-        return carry
 
     pltpu.make_async_copy(send.at[0], recv.at[0], a2a_r.at[0]).start()
-    lax.fori_loop(1, experts, dispatch, 0)
+    for r in range(1, experts):
+        if r == blocks:
+            pl.semaphore_wait(torus_sem, zs - 1)
+        remote(send.at[r], recv.at[r], a2a_s, a2a_r.at[r // blocks], peer(r, 1)).start()
 
     def span(j):
         return pl.ds(pl.multiple_of(j * rows, rows), rows)
@@ -285,15 +313,15 @@
         ret_out[pl.ds(j * blocks, blocks), 0:CAP, :] = split[:, :, 0 : feat // 2].astype(BF16)
         ret_out[pl.ds(j * blocks, blocks), CAP : 2 * CAP, :] = split[:, :, feat // 2 :].astype(BF16)
 
-        @pl.when(j == 0)
-        def _():
-            pltpu.make_async_copy(ret_out.at[0], ret_in.at[0], ret_r).start()
-
-        def back(r, carry):
-            remote(ret_out.at[r], ret_in.at[r], ret_s, ret_r, peer(r, -1)).start()
-            return carry
-
-        lax.fori_loop(jnp.maximum(j * blocks, 1), (j + 1) * blocks, back, 0)
+        for chunk in range(chunks):
+
+            @pl.when(j == chunk)
+            def _():
+                for r in range(chunk * blocks, (chunk + 1) * blocks):
+                    if r:
+                        remote(ret_out.at[r], ret_in.at[r], ret_s, ret_r, peer(r, -1)).start()
+                    else:
+                        pltpu.make_async_copy(ret_out.at[0], ret_in.at[0], ret_r).start()
 
     def step(i, carry):
         def stage(lag, work):
@@ -301,19 +329,19 @@
             def _():
                 work(i - lag)
 
-        stage(0, take_in)
-        stage(1, pass_near)
-        stage(2, pass_far)
-        stage(6, give_back)
-        stage(5, sum_near)
-        stage(4, sum_far)
-
-        @pl.when(i == 3)
+        stage(LAGS[0], take_in)
+        stage(LAGS[1], pass_near)
+        stage(LAGS[2], pass_far)
+
+        @pl.when(i == LAGS[3])
         def _():
             for fetch in fetches:
                 fetch.wait()
 
-        stage(3, multiply)
+        stage(LAGS[3], multiply)
+        stage(LAGS[4], sum_far)
+        stage(LAGS[5], sum_near)
+        stage(LAGS[6], give_back)
         return carry
 
     lax.fori_loop(0, iters, step, 0)
@@ -332,6 +360,8 @@
         lax.fori_loop(0, 2 * xs, column, 0)
         pltpu.make_async_copy(grads.at[m], outs[m].at[0], out_sem.at[m]).start()
 
+    slot_col = jnp.sum(jnp.where(row_i == col_i, slot, 0.0), axis=1, keepdims=True)
+    slot_col = slot_col.astype(jnp.int32)
     picking = jnp.where(
         lax.broadcasted_iota(jnp.int32, (tok_rows, rows_all), 1) == slot_col, 1.0, 0.0
     ).astype(BF16)
@@ -369,8 +399,9 @@
     slots = experts * CAP
     rows = slots // chunks
     whole = pl.BlockSpec(memory_space=pltpu.VMEM)
-    away = pl.BlockSpec(memory_space=pl.ANY)
+    away = pl.BlockSpec(memory_space=pltpu.HBM)
     dma = pltpu.SemaphoreType.DMA
+    hold = functools.partial(pltpu.with_memory_space_constraint, memory_space=pltpu.HBM)
     return pl.pallas_call(
         functools.partial(kernel, (zs, ys, xs, chunks)),
         out_shape=(
@@ -379,9 +410,12 @@
             jax.ShapeDtypeStruct(w_up.shape, BF16),
             jax.ShapeDtypeStruct(w_down.shape, BF16),
         ),
-        in_specs=[whole, whole, whole, away, away, away],
+        in_specs=[away] * 6,
         out_specs=(whole, away, away, away),
         scratch_shapes=[
+            pltpu.VMEM(tokens.shape, BF16),
+            pltpu.VMEM(upstream.shape, BF16),
+            pltpu.VMEM((1, tok_rows), jnp.int32),
             pltpu.VMEM((experts, 2 * CAP, feat), BF16),
             pltpu.VMEM((experts, 2 * CAP, feat), BF16),
             pltpu.VMEM((devices, 2, slots, feat), BF16),
@@ -397,6 +431,8 @@
             pltpu.VMEM((chunks, 2, rows, feat), BF16),
             pltpu.VMEM((experts, 2 * CAP, feat // 2), BF16),
             pltpu.VMEM((experts, 2 * CAP, feat // 2), BF16),
+            pltpu.SemaphoreType.REGULAR,
+            dma((3,)),
             dma((3,)),
             dma,
             dma((chunks,)),
@@ -411,7 +447,14 @@
         compiler_params=pltpu.CompilerParams(
             collective_id=0, has_side_effects=True, vmem_limit_bytes=48 * 1024 * 1024
         ),
-    )(tokens, upstream, expert_ids, w_gate, w_up, w_down)
+    )(
+        hold(tokens),
+        hold(upstream),
+        hold(expert_ids.reshape(1, tok_rows)),
+        hold(w_gate),
+        hold(w_up),
+        hold(w_down),
+    )
 
 
 def solution(mesh):

time: 83.5 us -> 69 us (0.83)
  the two profiles are of different devices: /device:TPU:8 before, /device:TPU:2 now
where the time goes in v3:
time: 69 us; the launch traced here: 68.9 us
  Pallas kernels  65 us (94%)
  local copies, waits for them, and re-layouts  3.23 us (5%)
    pallas_call x1, Pallas kernels, on_device(): pl.pallas_call(functools.partial(kernel, (zs, ys, xs, chunks)), out_shape...  65 us
    unnamed x4, local copies, waits for them, and re-layouts  3.23 us

profile of v3, /device:TPU:2, one launch (start us, length us, event | category | flops | bytes accessed | tf_op | source)
XLA Modules:
  0.0 68.9 jit_solution(7222777896583475349)
XLA Ops:
  0.6 65.0 %shard_map.93 = (bf16[256,256]{1,0:T(8,128)(2,1)S(1)}, bf16[1,176,2048]{2,1,0:T(8,128)(2,1)S(1)}, bf16[1,176,2048]{2,1,0:T(8,128)(2,1)S(1)}, bf16[1,176,2048]{2,1,0:T(8,128)(2,1)S(1)}) custom-call(bf16[256,256]{1,0:T(8,128)(2,1)} %tok_hbm.1, bf16[256,256]{1,0:T(8,128)(2,1)} %up_hbm.1, s32[1,256]{1,0:T(1,128)} %bitcast.1, bf16[1,176,2048]{2,1,0:T(8,128)(2,1)} %wg_hbm.1, ...), custom_call_target="tpu_custom_call" | custom-call | tf_op jit(solution)/shard_map/pallas_call | solution.py:405
  65.7 0.7 copy.14
  66.3 0.9 %copy.15 = bf16[1,176,2048]{2,1,0:T(8,128)(2,1)} copy(bf16[1,176,2048]{2,1,0:T(8,128)(2,1)S(1)} %get-tuple-element.9) | data formatting | bytes 1441792
  67.2 0.9 %copy.16 = bf16[1,176,2048]{2,1,0:T(8,128)(2,1)} copy(bf16[1,176,2048]{2,1,0:T(8,128)(2,1)S(1)} %get-tuple-element.10) | data formatting | bytes 1441792
  68.0 0.9 %copy.17 = bf16[1,176,2048]{2,1,0:T(8,128)(2,1)} copy(bf16[1,176,2048]{2,1,0:T(8,128)(2,1)S(1)} %get-tuple-element.11) | data formatting | bytes 1441792

commit v4 on v3

--- a/solution.py
+++ b/solution.py
@@ -13,7 +13,7 @@
 CAP = 8
 Y_SIDE = 8
 CHUNKS = 4
-LAGS = (0, 1, 2, 3, 4, 5, 6)
+LAGS = (0, 1, 2, 3, 4, 5, 7)
 
 
 def log2(value):
@@ -27,8 +27,7 @@
     pairs = sorted(((dz, dy) for dz in range(zs) for dy in range(ys)), key=far)
     ring = [pair for pair in pairs if 0 in pair]
     pairs = ring + [pair for pair in pairs if 0 not in pair]
-    rest = pairs[count:]
-    return pairs[:count] + rest[:count] + rest[2 * count :] + rest[count : 2 * count]
+    return pairs
 
 
 def kernel(
@@ -175,10 +174,14 @@
 
 
     pltpu.make_async_copy(send.at[0], recv.at[0], a2a_r.at[0]).start()
-    for r in range(1, experts):
-        if r == blocks:
-            pl.semaphore_wait(torus_sem, zs - 1)
-        remote(send.at[r], recv.at[r], a2a_s, a2a_r.at[r // blocks], peer(r, 1)).start()
+    def dispatch(chunk):
+        for r in reversed(range(max(chunk * blocks, 1), (chunk + 1) * blocks)):
+            remote(send.at[r], recv.at[r], a2a_s, a2a_r.at[chunk], peer(r, 1)).start()
+
+    dispatch(0)
+    pl.semaphore_wait(torus_sem, zs - 1)
+    for chunk in range(1, chunks - 1):
+        dispatch(chunk)
 
     def span(j):
         return pl.ds(pl.multiple_of(j * rows, rows), rows)
@@ -317,37 +320,18 @@
 
             @pl.when(j == chunk)
             def _():
-                for r in range(chunk * blocks, (chunk + 1) * blocks):
+                for r in reversed(range(chunk * blocks, (chunk + 1) * blocks)):
                     if r:
                         remote(ret_out.at[r], ret_in.at[r], ret_s, ret_r, peer(r, -1)).start()
                     else:
                         pltpu.make_async_copy(ret_out.at[0], ret_in.at[0], ret_r).start()
 
-    def step(i, carry):
-        def stage(lag, work):
-            @pl.when(jnp.logical_and(i >= lag, i < chunks + lag))
-            def _():
-                work(i - lag)
-
-        stage(LAGS[0], take_in)
-        stage(LAGS[1], pass_near)
-        stage(LAGS[2], pass_far)
-
-        @pl.when(i == LAGS[3])
-        def _():
-            for fetch in fetches:
-                fetch.wait()
-
-        stage(LAGS[3], multiply)
-        stage(LAGS[4], sum_far)
-        stage(LAGS[5], sum_near)
-        stage(LAGS[6], give_back)
-        return carry
-
-    lax.fori_loop(0, iters, step, 0)
-
     outs = (gg_ref, gu_ref, gd_ref)
-    for m in range(3):
+
+    def grad_copy(m):
+        return pltpu.make_async_copy(grads.at[m], outs[m].at[0], out_sem.at[m])
+
+    def grad(m):
         turned = acts[m].T
         side = 1 if m == 2 else 0
 
@@ -358,8 +342,36 @@
             return carry
 
         lax.fori_loop(0, 2 * xs, column, 0)
-        pltpu.make_async_copy(grads.at[m], outs[m].at[0], out_sem.at[m]).start()
-
+        grad_copy(m).start()
+
+    def step(i, carry):
+        def stage(lag, work, first=0):
+            @pl.when(jnp.logical_and(i >= lag + first, i < chunks + lag))
+            def _():
+                work(i - lag)
+
+        pl.when(i == 1)(functools.partial(pass_near, 0))
+        stage(LAGS[0], take_in)
+        pl.when(i == 1)(functools.partial(pass_far, 0))
+        pl.when(i == 0)(functools.partial(dispatch, chunks - 1))
+        stage(LAGS[1], pass_near, 1)
+        stage(LAGS[2], pass_far, 1)
+
+        @pl.when(i == LAGS[3])
+        def _():
+            for fetch in fetches:
+                fetch.wait()
+
+        stage(LAGS[3], multiply)
+        stage(LAGS[4], sum_far)
+        stage(LAGS[6], give_back)
+        stage(LAGS[5], sum_near)
+        return carry
+
+    lax.fori_loop(0, iters, step, 0)
+
+    for m in range(3):
+        grad(m)
     slot_col = jnp.sum(jnp.where(row_i == col_i, slot, 0.0), axis=1, keepdims=True)
     slot_col = slot_col.astype(jnp.int32)
     picking = jnp.where(
@@ -386,7 +398,7 @@
 
     lax.fori_loop(0, chunks, drain, 0)
     for m in range(3):
-        pltpu.make_async_copy(grads.at[m], outs[m].at[0], out_sem.at[m]).wait()
+        grad_copy(m).wait()
 
 
 def on_device(tokens, upstream, expert_ids, w_gate, w_up, w_down):

time: 69 us -> 67.8 us (0.983)
  the two profiles are of different devices: /device:TPU:2 before, /device:TPU:8 now
where the time goes in v4:
time: 67.8 us; the launch traced here: 67.6 us
  Pallas kernels  63.8 us (94%)
  local copies, waits for them, and re-layouts  3.23 us (5%)
    pallas_call x1, Pallas kernels, on_device(): pl.pallas_call(functools.partial(kernel, (zs, ys, xs, chunks)), out_shape...  63.8 us
    unnamed x4, local copies, waits for them, and re-layouts  3.23 us

profile of v4, /device:TPU:8, one launch (start us, length us, event | category | flops | bytes accessed | tf_op | source)
XLA Modules:
  0.0 67.6 jit_solution(4237735704901727523)
XLA Ops:
  0.6 63.8 %shard_map.93 = (bf16[256,256]{1,0:T(8,128)(2,1)S(1)}, bf16[1,176,2048]{2,1,0:T(8,128)(2,1)S(1)}, bf16[1,176,2048]{2,1,0:T(8,128)(2,1)S(1)}, bf16[1,176,2048]{2,1,0:T(8,128)(2,1)S(1)}) custom-call(bf16[256,256]{1,0:T(8,128)(2,1)} %tok_hbm.1, bf16[256,256]{1,0:T(8,128)(2,1)} %up_hbm.1, s32[1,256]{1,0:T(1,128)} %bitcast.1, bf16[1,176,2048]{2,1,0:T(8,128)(2,1)} %wg_hbm.1, ...), custom_call_target="tpu_custom_call" | custom-call | tf_op jit(solution)/shard_map/pallas_call | solution.py:417
  64.4 0.7 copy.14
  65.1 0.9 %copy.15 = bf16[1,176,2048]{2,1,0:T(8,128)(2,1)} copy(bf16[1,176,2048]{2,1,0:T(8,128)(2,1)S(1)} %get-tuple-element.9) | data formatting | bytes 1441792
  65.9 0.9 %copy.16 = bf16[1,176,2048]{2,1,0:T(8,128)(2,1)} copy(bf16[1,176,2048]{2,1,0:T(8,128)(2,1)S(1)} %get-tuple-element.10) | data formatting | bytes 1441792
  66.8 0.9 %copy.17 = bf16[1,176,2048]{2,1,0:T(8,128)(2,1)} copy(bf16[1,176,2048]{2,1,0:T(8,128)(2,1)S(1)} %get-tuple-element.11) | data formatting | bytes 1441792

commit v5 on v4

--- a/solution.py
+++ b/solution.py
@@ -352,7 +352,7 @@
 
         pl.when(i == 1)(functools.partial(pass_near, 0))
         stage(LAGS[0], take_in)
-        pl.when(i == 1)(functools.partial(pass_far, 0))
+        pl.when(i == 2)(functools.partial(pass_far, 0))
         pl.when(i == 0)(functools.partial(dispatch, chunks - 1))
         stage(LAGS[1], pass_near, 1)
         stage(LAGS[2], pass_far, 1)

time: 67.8 us -> 67.2 us (level)
  no operation moved by 1% of the time
where the time goes in v5:
time: 67.2 us; the launch traced here: 67.1 us
  Pallas kernels  63.2 us (94%)
  local copies, waits for them, and re-layouts  3.23 us (5%)
    pallas_call x1, Pallas kernels, on_device(): pl.pallas_call(functools.partial(kernel, (zs, ys, xs, chunks)), out_shape...  63.2 us
    unnamed x4, local copies, waits for them, and re-layouts  3.23 us

profile of v5, /device:TPU:8, one launch (start us, length us, event | category | flops | bytes accessed | tf_op | source)
XLA Modules:
  0.0 67.1 jit_solution(10030047395910688749)
XLA Ops:
  0.6 63.2 %shard_map.93 = (bf16[256,256]{1,0:T(8,128)(2,1)S(1)}, bf16[1,176,2048]{2,1,0:T(8,128)(2,1)S(1)}, bf16[1,176,2048]{2,1,0:T(8,128)(2,1)S(1)}, bf16[1,176,2048]{2,1,0:T(8,128)(2,1)S(1)}) custom-call(bf16[256,256]{1,0:T(8,128)(2,1)} %tok_hbm.1, bf16[256,256]{1,0:T(8,128)(2,1)} %up_hbm.1, s32[1,256]{1,0:T(1,128)} %bitcast.1, bf16[1,176,2048]{2,1,0:T(8,128)(2,1)} %wg_hbm.1, ...), custom_call_target="tpu_custom_call" | custom-call | tf_op jit(solution)/shard_map/pallas_call | solution.py:417
  63.9 0.7 copy.14
  64.5 0.9 %copy.15 = bf16[1,176,2048]{2,1,0:T(8,128)(2,1)} copy(bf16[1,176,2048]{2,1,0:T(8,128)(2,1)S(1)} %get-tuple-element.9) | data formatting | bytes 1441792
  65.4 0.9 %copy.16 = bf16[1,176,2048]{2,1,0:T(8,128)(2,1)} copy(bf16[1,176,2048]{2,1,0:T(8,128)(2,1)S(1)} %get-tuple-element.10) | data formatting | bytes 1441792
  66.2 0.9 %copy.17 = bf16[1,176,2048]{2,1,0:T(8,128)(2,1)} copy(bf16[1,176,2048]{2,1,0:T(8,128)(2,1)S(1)} %get-tuple-element.11) | data formatting | bytes 1441792
